TPU v7x, 32 devices: a whole 2x2x4 slice. The times are simulated.
32 devices in a mesh: shard: 4 (over y, x), ctx: 2 (over core), tp: 4 (over z).
Axes of the slice: x: 2, y: 2, z: 4, core: 2. Of those that a mesh axis runs over, the one named last changes fastest.
Arguments:
- tokens: bfloat16 [4, 1024, 1536], P('shard', ('ctx', 'tp')), may hold values from -6 to 6
- cotangent: bfloat16 [4, 1024, 1536], P('shard', ('ctx', 'tp')), may hold values from -6 to 6
- lengths: int32 [4], P('shard'), may hold values from 256 to 1024, as said below
- w_qkv: bfloat16 [1536, 3, 1536], P(('shard', 'ctx'), None, 'tp'), may hold values from -0.15625 to 0.15625
- w_forget: bfloat16 [1536, 24], P(('shard', 'ctx'), 'tp'), may hold values from -0.15625 to 0.15625
- forget_bias: float32 [24], replicated, may hold values from 3 to 8
- w_ogate: bfloat16 [1536, 1536], P(('shard', 'ctx'), 'tp'), may hold values from -0.15625 to 0.15625
- w_out: bfloat16 [1536, 1536], P(('shard', 'ctx'), 'tp'), may hold values from -0.625 to 0.625
- w_gu: bfloat16 [1536, 2, 4096], P(('shard', 'ctx'), None, 'tp'), may hold values from -0.15625 to 0.15625
- w_down: bfloat16 [1536, 4096], P(('shard', 'ctx'), 'tp'), may hold values from -0.09375 to 0.09375
- gain_attn: float32 [1536], replicated, may hold values from 0.5 to 1.5
- gain_mlp: float32 [1536], replicated, may hold values from 0.5 to 1.5
- qk_gain: float32 [2, 64], replicated, may hold values from 1 to 2
Outputs:
- output: bfloat16 [4, 1024, 1536], P('shard', ('ctx', 'tp'))
- input_grad: bfloat16 [4, 1024, 1536], P('shard', ('ctx', 'tp'))
- grad_qkv: float32 [1536, 3, 1536], P(('shard', 'ctx'), None, 'tp')
- grad_forget: float32 [1536, 24], P(('shard', 'ctx'), 'tp')
- grad_forget_bias: float32 [24], replicated
- grad_ogate: float32 [1536, 1536], P(('shard', 'ctx'), 'tp')
- grad_out: float32 [1536, 1536], P(('shard', 'ctx'), 'tp')
- grad_gu: float32 [1536, 2, 4096], P(('shard', 'ctx'), None, 'tp')
- grad_down: float32 [1536, 4096], P(('shard', 'ctx'), 'tp')
- grad_gain_attn: float32 [1536], replicated
- grad_gain_mlp: float32 [1536], replicated
- grad_qk_gain: float32 [2, 64], replicated
Inputs may be any that keep to these rules, and one draw needn't show every extreme that they name: `lengths`: real tokens of a slot; positions at or past it are padding; both the least and the most value occur in every draw.
All inputs are finite; a program needn't handle non-finite values.
Results may differ from a plain program's by a relative error of at most 0.04.
Values may be sent and summed in bfloat16 or wider, within the bound.
No kernel may reach another device: no remote copies, remote signals or barrier semaphores. Data moves between devices by JAX's collectives and lax.ppermute only.
A program may use at most 128 MiB of HBM per device.

v0:
```python
import math
import jax
import jax.numpy as jnp
from jax import lax
from jax.sharding import PartitionSpec as P

epsilon = 1e-06


def shifted(block, axis, distance):
    devices = range(lax.axis_size(axis))
    route = [(i - distance, i) for i in devices if i - distance in devices]
    return lax.ppermute(block, axis, route)


def norm_rows(values, gain):
    return values * lax.rsqrt(jnp.mean(values * values, axis=-1, keepdims=True) + epsilon) * gain


def product(left, right):
    return jnp.dot(left, right, preferred_element_type=jnp.float32)


def product_t(left, right):
    return lax.dot_general(
        left, right, (((1,), (1,)), ((), ())), preferred_element_type=jnp.float32
    )


def outer_rows(left, right):
    return lax.dot_general(
        left, right, (((0,), (0,)), ((), ())), preferred_element_type=jnp.float32
    )


def body(
    tokens,
    cotangent,
    lengths,
    w_qkv,
    w_forget,
    forget_bias,
    w_ogate,
    w_out,
    w_gu,
    w_down,
    gain_attn,
    gain_mlp,
    qk_gain,
):
    slot_count, own_rows, model_width = tokens.shape
    tensor_size = lax.axis_size("tp")
    tensor_place = lax.axis_index("tp")
    span_index = lax.axis_index("ctx")
    half_rows = own_rows * tensor_size
    row_count = slot_count * half_rows
    local_heads = w_forget.shape[1]
    head_size = qk_gain.shape[1]
    head_cols = local_heads * head_size
    hidden_units = w_down.shape[1]
    item_count = slot_count * local_heads
    score_scale = 1.0 / math.sqrt(head_size)
    own_start = tensor_place * own_rows
    full_tokens, full_cot = (
        lax.all_gather(tokens, "tp", axis=1, tiled=True),
        lax.all_gather(cotangent, "tp", axis=1, tiled=True),
    )
    qkv_full, forget_full, ogate_full, out_full, gu_full, down_full = (
        lax.all_gather(w_qkv, ("shard", "ctx"), axis=0, tiled=True),
        lax.all_gather(w_forget, ("shard", "ctx"), axis=0, tiled=True),
        lax.all_gather(w_ogate, ("shard", "ctx"), axis=0, tiled=True),
        lax.all_gather(w_out, ("shard", "ctx"), axis=0, tiled=True),
        lax.all_gather(w_gu, ("shard", "ctx"), axis=0, tiled=True),
        lax.all_gather(w_down, ("shard", "ctx"), axis=0, tiled=True),
    )
    qkv_flat = qkv_full.reshape(model_width, 3 * head_cols)
    gu_flat = gu_full.reshape(model_width, 2 * hidden_units)

    def own_slice(values):
        return lax.dynamic_slice_in_dim(
            values.reshape(slot_count, half_rows, values.shape[-1]), own_start, own_rows, 1
        )

    positions = span_index * half_rows + jnp.arange(half_rows, dtype=jnp.int32)
    valid_rows = (positions[None, :] < lengths[:, None]).astype(jnp.float32).reshape(row_count, 1)
    own_positions = span_index * half_rows + own_start + jnp.arange(own_rows, dtype=jnp.int32)
    valid_own = (own_positions[None, :] < lengths[:, None]).astype(jnp.float32)[:, :, None]
    residual = full_tokens.reshape(row_count, model_width).astype(jnp.float32)
    normed = norm_rows(residual, gain_attn).astype(jnp.bfloat16)
    qkv_rows = product(normed, qkv_flat).reshape(row_count, 3, head_cols)
    query_raw = qkv_rows[:, 0].reshape(row_count, local_heads, head_size)
    key_raw = qkv_rows[:, 1].reshape(row_count, local_heads, head_size)
    queries = (
        norm_rows(query_raw, qk_gain[0])
        .astype(jnp.bfloat16)
        .reshape(slot_count, half_rows, head_cols)
    )
    keys_here = (
        norm_rows(key_raw, qk_gain[1])
        .astype(jnp.bfloat16)
        .reshape(slot_count, half_rows, head_cols)
    )
    values_here = qkv_rows[:, 2].astype(jnp.bfloat16).reshape(slot_count, half_rows, head_cols)
    bias_here = lax.dynamic_slice_in_dim(forget_bias, tensor_place * local_heads, local_heads)
    forget_pre = (product(normed, forget_full) + bias_here).reshape(
        slot_count, half_rows, local_heads
    )
    cum_here = jnp.cumsum(jax.nn.log_sigmoid(forget_pre), axis=1)
    keys_left, values_left = shifted((keys_here, values_here), "ctx", 1)
    cum_left = shifted(cum_here, "ctx", 1)
    cum_query = cum_here + cum_left[:, -1:, :]

    def by_head(values):
        shaped = values.reshape(slot_count, half_rows, local_heads, head_size)
        return jnp.transpose(shaped, (0, 2, 1, 3)).reshape(item_count, half_rows, head_size)

    def by_head_cum(values):
        return jnp.transpose(values, (0, 2, 1)).reshape(item_count, half_rows)

    def to_slots(values):
        shaped = values.reshape(slot_count, local_heads, half_rows, head_size)
        return jnp.transpose(shaped, (0, 2, 1, 3)).reshape(slot_count, half_rows, head_cols)

    def to_slots_cum(values):
        return jnp.transpose(values.reshape(slot_count, local_heads, half_rows), (0, 2, 1))

    q_items = by_head(queries)
    k_items = jnp.concatenate([by_head(keys_left), by_head(keys_here)], axis=1)
    v_items = jnp.concatenate([by_head(values_left), by_head(values_here)], axis=1)
    cq_items = by_head_cum(cum_query)
    ck_items = jnp.concatenate([by_head_cum(cum_left), cq_items], axis=1)
    place_ids = jnp.arange(half_rows, dtype=jnp.int32)
    earlier = jnp.broadcast_to(span_index > 0, (half_rows, half_rows))
    allowed = jnp.concatenate([earlier, place_ids[None, :] <= place_ids[:, None]], axis=1)

    def score_block(query_block, key_block, cum_rows, cum_cols):
        score_raw = (
            product_t(query_block, key_block) * score_scale + cum_rows[:, None] - cum_cols[None, :]
        )
        return jnp.where(allowed, score_raw, -jnp.inf)

    def forward_item(pieces):
        query_block, key_block, value_block, cum_rows, cum_cols = pieces
        score_vals = score_block(query_block, key_block, cum_rows, cum_cols)
        row_max = jnp.max(score_vals, axis=1, keepdims=True)
        expo = jnp.exp(score_vals - row_max)
        row_total = jnp.sum(expo, axis=1, keepdims=True)
        attn_probs = (expo / row_total).astype(jnp.bfloat16)
        return (product(attn_probs, value_block), (row_max + jnp.log(row_total))[:, 0])

    attended_items, lse_items = lax.map(
        forward_item, (q_items, k_items, v_items, cq_items, ck_items)
    )
    attended_rows = to_slots(attended_items).reshape(row_count, head_cols)
    opener = jax.nn.sigmoid(product(normed, ogate_full))
    gated = (attended_rows * opener).astype(jnp.bfloat16)
    branch_part = product_t(gated, out_full)
    branch_full = lax.psum(branch_part, "tp")
    middle = residual + branch_full
    middle_share = own_slice(middle)
    normed_mid = norm_rows(middle, gain_mlp).astype(jnp.bfloat16)
    both = product(normed_mid, gu_flat).reshape(row_count, 2, hidden_units)
    gate_pre = both[:, 0]
    up_pre = both[:, 1]
    gate_sig = jax.nn.sigmoid(gate_pre)
    hidden = (gate_pre * gate_sig * up_pre).astype(jnp.bfloat16)
    down_share = lax.psum_scatter(
        product_t(hidden, down_full)
        .reshape(slot_count, half_rows, model_width)
        .astype(jnp.bfloat16),
        "tp",
        scatter_dimension=1,
        tiled=True,
    ).astype(jnp.float32)
    output = (valid_own * (middle_share + down_share)).astype(jnp.bfloat16)
    cot_rows = full_cot.reshape(row_count, model_width) * valid_rows.astype(jnp.bfloat16)
    d_hidden = product(cot_rows, down_full)
    d_gate = d_hidden * up_pre * gate_sig * (1.0 + gate_pre * (1.0 - gate_sig))
    d_up = d_hidden * gate_pre * gate_sig
    d_both = (
        jnp.stack([d_gate, d_up], axis=1).astype(jnp.bfloat16).reshape(row_count, 2 * hidden_units)
    )
    grad_down = outer_rows(cot_rows, hidden)
    grad_gu = outer_rows(normed_mid, d_both).reshape(model_width, 2, hidden_units)
    d_mid_terms = product_t(d_both, gu_flat)
    d_normed_mid = lax.psum(d_mid_terms, "tp")
    _, pull_mid = jax.vjp(norm_rows, middle, gain_mlp)
    d_middle_norm, d_gain_mlp_all = pull_mid(d_normed_mid)
    d_middle = d_middle_norm + cot_rows.astype(jnp.float32)
    feat_share = model_width // tensor_size
    owner = jnp.arange(model_width, dtype=jnp.int32) // feat_share == tensor_place
    d_gain_mlp_own = jnp.where(owner, d_gain_mlp_all, 0.0)
    d_branch = d_middle.astype(jnp.bfloat16)
    d_middle_share = own_slice(d_middle)
    d_gated = product(d_branch, out_full)
    grad_out = outer_rows(d_branch, gated)
    d_attended = (d_gated * opener).astype(jnp.bfloat16)
    d_open = (d_gated * attended_rows * opener * (1.0 - opener)).astype(jnp.bfloat16)
    grad_ogate = outer_rows(normed, d_open)
    da_items = by_head(d_attended.reshape(slot_count, half_rows, head_cols))

    def backward_item(pieces):
        query_block, key_block, value_block, cum_rows, cum_cols, lse_block, grad_block = pieces
        score_vals = score_block(query_block, key_block, cum_rows, cum_cols)
        attn_probs = jnp.exp(score_vals - lse_block[:, None])
        d_probs = product_t(grad_block, value_block)
        centre = jnp.sum(attn_probs * d_probs, axis=1, keepdims=True)
        d_scores = (attn_probs * (d_probs - centre)).astype(jnp.bfloat16)
        d_query_block = product(d_scores, key_block) * score_scale
        d_key_block = outer_rows(d_scores, query_block) * score_scale
        d_value_block = outer_rows(attn_probs.astype(jnp.bfloat16), grad_block)
        d_cum_rows = jnp.sum(d_scores, axis=1, dtype=jnp.float32)
        d_cum_cols = -jnp.sum(d_scores, axis=0, dtype=jnp.float32)
        return (d_query_block, d_key_block, d_value_block, d_cum_rows, d_cum_cols)

    dq_items, dk_items, dv_items, dcq_items, dck_items = lax.map(
        backward_item, (q_items, k_items, v_items, cq_items, ck_items, lse_items, da_items)
    )
    dc_own = dcq_items + dck_items[:, half_rows:]
    dc_left = dck_items[:, :half_rows]
    dc_left = dc_left.at[:, -1].add(jnp.sum(dc_own, axis=1))
    back_keys, back_values, back_cum = (
        shifted(to_slots(dk_items[:, :half_rows]).astype(jnp.bfloat16), "ctx", -1).astype(
            jnp.float32
        ),
        shifted(to_slots(dv_items[:, :half_rows]).astype(jnp.bfloat16), "ctx", -1).astype(
            jnp.float32
        ),
        shifted(to_slots_cum(dc_left).astype(jnp.bfloat16), "ctx", -1).astype(jnp.float32),
    )
    d_query = to_slots(dq_items).reshape(row_count, local_heads, head_size)
    d_key = (to_slots(dk_items[:, half_rows:]) + back_keys).reshape(
        row_count, local_heads, head_size
    )
    d_value = (to_slots(dv_items[:, half_rows:]) + back_values).reshape(row_count, head_cols)
    d_cum = to_slots_cum(dc_own) + back_cum
    d_log = jnp.flip(jnp.cumsum(jnp.flip(d_cum, 1), axis=1), 1)
    d_forget = d_log * jax.nn.sigmoid(-forget_pre)
    d_bias_own = jnp.sum(d_forget, axis=(0, 1))
    d_forget_low = d_forget.reshape(row_count, local_heads).astype(jnp.bfloat16)
    grad_forget = outer_rows(normed, d_forget_low)
    _, pull_query = jax.vjp(norm_rows, query_raw, qk_gain[0])
    d_query_raw, d_query_gain = pull_query(d_query)
    _, pull_key = jax.vjp(norm_rows, key_raw, qk_gain[1])
    d_key_raw, d_key_gain = pull_key(d_key)
    d_mixed = (
        jnp.stack(
            [
                d_query_raw.reshape(row_count, head_cols),
                d_key_raw.reshape(row_count, head_cols),
                d_value,
            ],
            axis=1,
        )
        .astype(jnp.bfloat16)
        .reshape(row_count, 3 * head_cols)
    )
    grad_qkv = outer_rows(normed, d_mixed).reshape(model_width, 3, head_cols)
    d_normed = (
        product_t(d_mixed, qkv_flat)
        + product_t(d_open, ogate_full)
        + product_t(d_forget_low, forget_full)
    )
    root = lax.rsqrt(jnp.mean(residual * residual, axis=1, keepdims=True) + epsilon)
    unit = residual * root
    d_unit = d_normed * gain_attn
    dot_part = (jnp.sum(d_unit * unit, axis=1) / model_width).reshape(slot_count, half_rows)
    d_unit_share, dot_full = (
        lax.psum_scatter(
            d_unit.reshape(slot_count, half_rows, model_width).astype(jnp.bfloat16),
            "tp",
            scatter_dimension=1,
            tiled=True,
        ).astype(jnp.float32),
        lax.psum_scatter(
            dot_part.astype(jnp.bfloat16), "tp", scatter_dimension=1, tiled=True
        ).astype(jnp.float32),
    )
    unit_share = own_slice(unit)
    root_share = own_slice(root)
    input_grad = (
        d_middle_share + root_share * (d_unit_share - unit_share * dot_full[:, :, None])
    ).astype(jnp.bfloat16)
    grad_parts = (
        lax.psum_scatter(
            grad_qkv.astype(jnp.bfloat16), ("shard", "ctx"), scatter_dimension=0, tiled=True
        ).astype(jnp.float32),
        lax.psum_scatter(
            grad_forget.astype(jnp.bfloat16), ("shard", "ctx"), scatter_dimension=0, tiled=True
        ).astype(jnp.float32),
        lax.psum_scatter(
            grad_ogate.astype(jnp.bfloat16), ("shard", "ctx"), scatter_dimension=0, tiled=True
        ).astype(jnp.float32),
        lax.psum_scatter(
            grad_out.astype(jnp.bfloat16), ("shard", "ctx"), scatter_dimension=0, tiled=True
        ).astype(jnp.float32),
        lax.psum_scatter(
            grad_gu.astype(jnp.bfloat16), ("shard", "ctx"), scatter_dimension=0, tiled=True
        ).astype(jnp.float32),
        lax.psum_scatter(
            grad_down.astype(jnp.bfloat16), ("shard", "ctx"), scatter_dimension=0, tiled=True
        ).astype(jnp.float32),
    )
    bias_full = lax.dynamic_update_slice_in_dim(
        jnp.zeros(forget_bias.shape, jnp.float32), d_bias_own, tensor_place * local_heads, 0
    )
    gain_attn_part = jnp.sum(d_normed * unit, axis=0)
    small_parts = lax.psum(
        (gain_attn_part, d_gain_mlp_own, jnp.stack([d_query_gain, d_key_gain]), bias_full),
        ("shard", "ctx", "tp"),
    )
    return (
        output,
        input_grad,
        grad_parts[0],
        grad_parts[1],
        small_parts[3],
        grad_parts[2],
        grad_parts[3],
        grad_parts[4],
        grad_parts[5],
        small_parts[0],
        small_parts[1],
        small_parts[2],
    )


def solution(mesh):
    return jax.shard_map(
        body,
        mesh=mesh,
        in_specs=(
            P("shard", ("ctx", "tp"), None),
            P("shard", ("ctx", "tp"), None),
            P("shard"),
            P(("shard", "ctx"), None, "tp"),
            P(("shard", "ctx"), "tp"),
            P(),
            P(("shard", "ctx"), "tp"),
            P(("shard", "ctx"), "tp"),
            P(("shard", "ctx"), None, "tp"),
            P(("shard", "ctx"), "tp"),
            P(),
            P(),
            P(),
        ),
        out_specs=(
            P("shard", ("ctx", "tp"), None),
            P("shard", ("ctx", "tp"), None),
            P(("shard", "ctx"), None, "tp"),
            P(("shard", "ctx"), "tp"),
            P(),
            P(("shard", "ctx"), "tp"),
            P(("shard", "ctx"), "tp"),
            P(("shard", "ctx"), None, "tp"),
            P(("shard", "ctx"), "tp"),
            P(),
            P(),
            P(),
        ),
        check_vma=False,
    )
```

profile of v0, /device:TPU:0, one launch (start us, length us, event | category | flops | bytes accessed | tf_op | source)
XLA Modules:
  0.0 1049.7 jit_solution(11627350117377922482)
XLA Ops:
  11.9 10.6 %all-gather = bf16[8,192,6]{1,2,0:T(8,128)(2,1)S(1)} all-gather(bf16[1,192,6]{1,2,0:T(8,128)(2,1)} %bitcast.510), channel_id=1, replica_groups=mesh['shard'=4,'ctx'=2,'tp'=4] {'shard','ctx'}, dimensions={0}, use_global_device_ids=true | all-gather | bytes 20736 | tf_op jit(solution)/shard_map/all_gather | solution.py:70
  24.6 24.8 %all-gather.9.cloned.1.call-done = bf16[1,512,1536]{2,1,0:T(8,128)(2,1)} async-done(((bf16[1,128,1536]{2,1,0:T(8,128)(2,1)}), bf16[1,512,1536]{2,1,0:T(8,128)(2,1)}) %all-gather.9.cloned.1.call-update) | async-done | bytes 1572880 | tf_op jit(solution)/shard_map/all_gather | solution.py:65
  59.5 24.7 %all-gather.11.cloned.1.call-done = bf16[1536,3,384]{2,0,1:T(8,128)(2,1)} async-done(((bf16[192,3,384]{2,0,1:T(8,128)(2,1)}), bf16[1536,3,384]{2,0,1:T(8,128)(2,1)}) %all-gather.11.cloned.1.call-update) | async-done | bytes 3538960 | tf_op jit(solution)/shard_map/all_gather | solution.py:69
  84.2 6.1 copy.92
  90.3 4.1 fusion.41
  96.7 2.9 collective-permute-start
  106.8 3.3 fusion.74
  118.7 37.0 %while.31 = (s32[]{:T(128)}, f32[6,512,64]{1,2,0:T(8,128)}, f32[6,512]{1,0:T(8,128)S(1)}, bf16[6,512,64]{2,1,0:T(8,128)(2,1)}, bf16[6,1024,64]{2,1,0:T(8,128)(2,...) while((s32[]{:T(128)}, f32[6,512,64]{1,2,0:T(8,128)}, ...), condition=%wide.region_8.9_spmd, body=%wide.region_5.8_spmd.sunk | while | flops 139460096 | bytes 7643265 | solution.py:151
  128.7 2.3 fusion.162
  134.9 2.2 fusion.162
  156.2 3.4 fusion.84
  159.7 4.0 fusion.126
  168.9 116.0 %all-reduce.5.cloned.1.call-done = f32[512,1536]{1,0:T(8,128)} async-done(((f32[512,1536]{1,0:T(8,128)}), f32[512,1536]{1,0:T(8,128)}) %all-reduce.5.cloned.1.call-update) | async-done | bytes 3145744 | tf_op jit(solution)/shard_map/psum | solution.py:158
  284.9 2.8 multiply_reduce_fusion.5
  289.3 42.5 %all-gather.17.cloned.1.call-done = bf16[1536,2,1024]{2,0,1:T(8,128)(2,1)} async-done(((bf16[192,2,1024]{2,0,1:T(8,128)(2,1)}), bf16[1536,2,1024]{2,0,1:T(8,128)(2,1)}) %all-gather.17.cloned.1.call-update) | async-done | bytes 6291472 | tf_op jit(solution)/shard_map/all_gather | solution.py:73
  331.8 8.7 copy.104
  340.5 8.1 fusion.36
  348.6 21.9 %all-gather.21.cloned.1.call-done = bf16[1,512,1536]{2,1,0:T(8,128)(2,1)} async-done(((bf16[1,128,1536]{2,1,0:T(8,128)(2,1)}), bf16[1,512,1536]{2,1,0:T(8,128)(2,1)}) %all-gather.21.cloned.1.call-update) | async-done | bytes 1572880 | tf_op jit(solution)/shard_map/all_gather | solution.py:66
  370.5 33.1 %all-gather.19.cloned.1.call-done = bf16[1536,1024]{1,0:T(8,128)(2,1)} async-done(((bf16[192,1024]{1,0:T(8,128)(2,1)}), bf16[1536,1024]{1,0:T(8,128)(2,1)}) %all-gather.19.cloned.1.call-update) | async-done | bytes 3145744 | tf_op jit(solution)/shard_map/all_gather | solution.py:74
  403.6 5.9 fusion.52
  410.9 8.0 convolution_bitcast_fusion.2
  423.5 6.7 fusion.47
  430.5 109.7 %all-reduce.7.cloned.1.call-done = f32[512,1536]{1,0:T(8,128)} async-done(((f32[512,1536]{1,0:T(8,128)}), f32[512,1536]{1,0:T(8,128)}) %all-reduce.7.cloned.1.call-update) | async-done | bytes 3145744 | tf_op jit(solution)/shard_map/psum | solution.py:186
  540.2 3.4 multiply_reduce_fusion.1
  543.7 3.0 fusion.46
  552.2 97.2 %while.32 = (s32[]{:T(128)}, f32[6,512,64]{1,2,0:T(8,128)}, f32[6,1024,64]{1,2,0:T(8,128)}, f32[6,1024,64]{1,2,0:T(8,128)}, f32[6,512]{1,0:T(8,128)}, /*index=5*...) while((s32[]{:T(128)}, f32[6,512,64]{1,2,0:T(8,128)}, ...), condition=%wide.region_18.19_spmd, body=%wide.region_14.18_spmd.sunk | while | flops 342981632 | bytes 20376776 | solution.py:216
  667.2 2.3 fusion.80
  672.4 2.7 rev.7
  676.4 4.1 reduce-window.16
  691.2 2.7 rev.8
  695.9 2.6 convolution_convert_fusion.6
  700.6 2.3 multiply_reduce_fusion.6
  707.6 2.3 convolution_bitcast_fusion.3
  711.4 3.4 multiply_reduce_fusion.2
  715.7 6.4 convolution_convert_fusion.2
  722.2 3.7 convolution_convert_fusion.5
  729.0 5.8 convolution_convert_fusion.1
  734.9 3.1 maximum_convert_fusion
  738.0 4.0 copy.114
  742.0 8.9 convolution_convert_fusion
  755.5 41.1 %all-reduce.1 = (f32[24]{0:T(128)}, f32[1536]{0:T(1024)}, f32[1536]{0:T(1024)}, f32[2,64]{1,0:T(2,128)}) all-reduce(f32[24]{0:T(128)S(1)} %dynamic_update_slice.28, f32[1536]{0:T(1024)S(1)} %get-tuple-element.207, f32[1536]{0:T(1024)S(1)} %fusion.108, ...), channel_id=1, replica_groups=mesh['shard'=4,'ctx'=2,'tp'=4] {'shard','ctx','tp'}, use_global_device_ids=true, to_apply=%region_30.31 | all-reduce | flops 3224 | bytes 25792 | tf_op jit(solution)/shard_map/psum | solution.py:308
  797.5 8.2 reduce-scatter.26.cloned.1.call-done
  807.7 37.9 %reduce-scatter.20.cloned.1.call-done = bf16[192,384]{1,0:T(8,128)(2,1)} async-done(((bf16[1536,384]{1,0:T(8,128)(2,1)}), bf16[192,384]{1,0:T(8,128)(2,1)}) %reduce-scatter.20.cloned.1.call-update) | async-done | bytes 147472 | tf_op jit(solution)/shard_map/reduce_scatter | solution.py:291
  847.2 38.6 %reduce-scatter.22.cloned.1.call-done = bf16[192,384]{1,0:T(8,128)(2,1)} async-done(((bf16[1536,384]{1,0:T(8,128)(2,1)}), bf16[192,384]{1,0:T(8,128)(2,1)}) %reduce-scatter.22.cloned.1.call-update) | async-done | bytes 147472 | tf_op jit(solution)/shard_map/reduce_scatter | solution.py:294
  887.5 36.4 %reduce-scatter.16.cloned.1.call-done = bf16[1,128,1536]{2,1,0:T(8,128)(2,1)} async-done(((bf16[1,512,1536]{2,1,0:T(8,128)(2,1)}), bf16[1,128,1536]{2,1,0:T(8,128)(2,1)}) %reduce-scatter.16.cloned.1.call-update) | async-done | bytes 393232 | tf_op jit(solution)/shard_map/reduce_scatter | solution.py:269
  926.1 48.2 %reduce-scatter.18.cloned.1.call-done = bf16[192,3,384]{2,0,1:T(8,128)(2,1)} async-done(((bf16[1536,3,384]{2,0,1:T(8,128)(2,1)}), bf16[192,3,384]{2,0,1:T(8,128)(2,1)}) %reduce-scatter.18.cloned.1.call-update) | async-done | bytes 442384 | tf_op jit(solution)/shard_map/reduce_scatter | solution.py:285
  976.3 63.0 %reduce-scatter.24.cloned.1.call-done = bf16[192,2,1024]{2,0,1:T(8,128)(2,1)} async-done(((bf16[1536,2,1024]{2,0,1:T(8,128)(2,1)}), bf16[192,2,1024]{2,0,1:T(8,128)(2,1)}) %reduce-scatter.24.cloned.1.call-update) | async-done | bytes 786448 | tf_op jit(solution)/shard_map/reduce_scatter | solution.py:297
  1039.3 3.1 copy.116
  (419 shorter events, 243.9 us)
Async XLA Ops:
  7.2 17.4 %copy-start.69 = (f32[24]{0:T(128)S(1)}, f32[24]{0:T(128)}, u32[]{:S(2)}) copy-start(f32[24]{0:T(128)} %param.24) | copy-start | bytes 292
  7.2 42.2 %all-gather.9.cloned.1.call-start = ((), (), s32[]{:S(2)}) async-start(), calls=%async_computation.9 | async-start | bytes 1966080 | tf_op jit(solution)/shard_map/all_gather | solution.py:65
  7.9 76.3 %all-gather.11.cloned.1.call-start = ((), (), s32[]{:S(2)}) async-start(), calls=%async_computation.10 | async-start | bytes 3981312 | tf_op jit(solution)/shard_map/all_gather | solution.py:69
  8.7 42.5 %copy-start.59 = (f32[1536]{0:T(1024)S(1)}, f32[1536]{0:T(1024)}, u32[]{:S(2)}) copy-start(f32[1536]{0:T(1024)} %param.29) | copy-start | bytes 18436
  8.7 147.0 %all-gather.13.cloned.1.call-start = ((), (), s32[]{:S(2)}) async-start(), calls=%async_computation.11 | async-start | bytes 1327104 | tf_op jit(solution)/shard_map/all_gather | solution.py:71
  9.4 150.3 %all-gather.15.cloned.1.call-start = ((), (), s32[]{:S(2)}) async-start(), calls=%async_computation.12 | async-start | bytes 1327104 | tf_op jit(solution)/shard_map/all_gather | solution.py:72
  10.0 274.9 %all-reduce.5.cloned.1.call-start = ((), (), s32[]{:S(2)}) async-start(), calls=%async_computation.13 | async-start | bytes 6291456 | tf_op jit(solution)/shard_map/psum | solution.py:158
  11.5 84.3 %copy-start.49 = (f32[384]{0:T(512)}, f32[384]{0:T(512)S(1)}, u32[]{:S(2)}) copy-start(f32[384]{0:T(512)S(1)} %mul.513) | copy-start | bytes 4612
  22.7 30.5 %copy-start.39 = (bf16[1536,6]{0,1:T(8,128)(2,1)}, bf16[1536,6]{0,1:T(8,128)(2,1)S(1)}, u32[]{:S(2)}) copy-start(bf16[1536,6]{0,1:T(8,128)(2,1)S(1)} %reshape.771) | copy-start | bytes 55300
  51.2 39.1 %copy-start.57 = (f32[512]{0:T(512)}, f32[512]{0:T(512)S(1)}, u32[]{:S(2)}) copy-start(f32[512]{0:T(512)S(1)} %add_rsqrt_fusion) | copy-start | bytes 6148
  53.2 5.0 copy-start.42
  55.5 2.4 collective-permute-start.1
  59.5 30.8 %copy-start.2 = (bf16[1,512,1536]{2,1,0:T(8,128)(2,1)S(1)}, bf16[1,512,1536]{2,1,0:T(8,128)(2,1)}, u32[]{:S(2)}) copy-start(bf16[1,512,1536]{2,1,0:T(8,128)(2,1)} %all-gather.9.cloned.1.call-done) | copy-start | bytes 4718596
  94.4 7.8 copy-start.4
  94.6 7.8 copy-start.9
  94.6 9.4 copy-start.6
  95.7 6.0 copy-start.37
  95.8 5.9 copy-start.35
  96.7 13.4 %collective-permute-start = (bf16[1,512,384]{1,2,0:T(8,128)(2,1)}, bf16[1,512,384]{1,2,0:T(8,128)(2,1)}, u32[]{:S(2)}, u32[]{:S(2)}) collective-permute-start(bf16[1,512,384]{1,2,0:T(8,128)(2,1)} %multiply_convert_fusion.9), channel_id=1, source_target_pairs={{0,4},{1,5},{2,6},{3,7},{8,12},{9,13},{10,14},{11,15},{16,20},{17,... | collective-permute-start | bytes 1179656 | tf_op jit(solution)/shard_map/ppermute | solution.py:13
  99.6 12.7 %collective-permute-start.2 = (bf16[1,512,384]{1,2,0:T(8,128)(2,1)}, bf16[1,512,384]{1,2,0:T(8,128)(2,1)}, u32[]{:S(2)}, u32[]{:S(2)}) collective-permute-start(bf16[1,512,384]{1,2,0:T(8,128)(2,1)} %slice_bitcast_fusion.5), channel_id=1, source_target_pairs={{0,4},{1,5},{2,6},{3,7},{8,12},{9,13},{10,14},{11,15},{16,20},{17,... | collective-permute-start | bytes 1179656 | tf_op jit(solution)/shard_map/ppermute | solution.py:13
  155.6 4.0 copy-start.10
  163.7 168.1 %all-gather.17.cloned.1.call-start = ((), (), s32[]{:S(2)}) async-start(), calls=%async_computation.14 | async-start | bytes 7077888 | tf_op jit(solution)/shard_map/all_gather | solution.py:73
  165.9 204.6 %all-gather.21.cloned.1.call-start = ((), (), s32[]{:S(2)}) async-start(), calls=%async_computation.17 | async-start | bytes 1966080 | tf_op jit(solution)/shard_map/all_gather | solution.py:66
  166.7 236.9 %all-gather.19.cloned.1.call-start = ((), (), s32[]{:S(2)}) async-start(), calls=%async_computation.15 | async-start | bytes 3538944 | tf_op jit(solution)/shard_map/all_gather | solution.py:74
  167.4 372.7 %all-reduce.7.cloned.1.call-start = ((), (), s32[]{:S(2)}) async-start(), calls=%async_computation.18 | async-start | bytes 6291456 | tf_op jit(solution)/shard_map/psum | solution.py:186
  287.8 252.4 %copy-start = (f32[512,1536]{1,0:T(8,128)}, f32[512,1536]{1,0:T(8,128)S(1)}, u32[]{:S(2)}) copy-start(f32[512,1536]{1,0:T(8,128)S(1)} %get-tuple-element.267) | copy-start | bytes 9437188
  418.9 332.6 %reduce-scatter.14.cloned.1.call-start = ((), (), s32[]{:S(2)}) async-start(), calls=%async_computation.16 | async-start | bytes 1966080 | tf_op jit(solution)/shard_map/reduce_scatter | solution.py:167
  430.2 323.7 %reduce-scatter.30.cloned.1.call-start = ((), (), s32[]{:S(2)}) async-start(), calls=%async_computation.26 | async-start | bytes 442368
  653.4 51.8 %collective-permute-start.4 = (bf16[1,512,384]{1,2,0:T(8,128)(2,1)}, bf16[1,512,384]{1,2,0:T(8,128)(2,1)}, u32[]{:S(2)}, u32[]{:S(2)}) collective-permute-start(bf16[1,512,384]{1,2,0:T(8,128)(2,1)} %bitcast.100), channel_id=1, source_target_pairs={{4,0},{5,1},{6,2},{7,3},{12,8},{13,9},{14,10},{15,11},{20,16},{21,... | collective-permute-start | bytes 1179656 | tf_op jit(solution)/shard_map/ppermute | solution.py:13
  656.6 44.0 %collective-permute-start.3 = (bf16[1,512,384]{1,2,0:T(8,128)(2,1)}, bf16[1,512,384]{1,2,0:T(8,128)(2,1)}, u32[]{:S(2)}, u32[]{:S(2)}) collective-permute-start(bf16[1,512,384]{1,2,0:T(8,128)(2,1)} %bitcast.90), channel_id=1, source_target_pairs={{4,0},{5,1},{6,2},{7,3},{12,8},{13,9},{14,10},{15,11},{20,16},{21,... | collective-permute-start | bytes 1179656 | tf_op jit(solution)/shard_map/ppermute | solution.py:13
  665.8 5.1 copy-start.24
  665.8 6.0 copy-start.34
  665.8 6.0 copy-start.38
  665.8 6.0 collective-permute-start.5
  700.3 96.4 %reduce-scatter.28.cloned.1.call-start = ((), (), s32[]{:S(2)}) async-start(), calls=%async_computation.25 | async-start | bytes 163840
  705.2 4.7 copy-start.27
  705.2 4.7 copy-start.29
  711.4 4.3 copy-start.66
  715.7 90.0 %reduce-scatter.26.cloned.1.call-start = ((), (), s32[]{:S(2)}) async-start(), calls=%async_computation.24 | async-start | bytes 3538944 | tf_op jit(solution)/shard_map/reduce_scatter | solution.py:300
  722.2 123.4 %reduce-scatter.20.cloned.1.call-start = ((), (), s32[]{:S(2)}) async-start(), calls=%async_computation.21 | async-start | bytes 1327104 | tf_op jit(solution)/shard_map/reduce_scatter | solution.py:291
  725.9 159.9 %reduce-scatter.22.cloned.1.call-start = ((), (), s32[]{:S(2)}) async-start(), calls=%async_computation.22 | async-start | bytes 1327104 | tf_op jit(solution)/shard_map/reduce_scatter | solution.py:294
  728.0 195.8 %reduce-scatter.16.cloned.1.call-start = ((), (), s32[]{:S(2)}) async-start(), calls=%async_computation.19 | async-start | bytes 1966080 | tf_op jit(solution)/shard_map/reduce_scatter | solution.py:269
  728.6 245.7 %reduce-scatter.18.cloned.1.call-start = ((), (), s32[]{:S(2)}) async-start(), calls=%async_computation.20 | async-start | bytes 3981312 | tf_op jit(solution)/shard_map/reduce_scatter | solution.py:285
  734.9 304.4 %reduce-scatter.24.cloned.1.call-start = ((), (), s32[]{:S(2)}) async-start(), calls=%async_computation.23 | async-start | bytes 7077888 | tf_op jit(solution)/shard_map/reduce_scatter | solution.py:297
  738.0 4.0 copy-start.45
  738.0 4.0 copy-start.52
  750.8 4.6 copy-start.56
  750.9 4.7 copy-start.67
  (51 other events, 109.9 us)
Sparse Core Ops, SparseCore 0:
  9.6 39.7 all-gather.8
  51.3 32.8 all-gather.10
  86.1 24.0 all-gather.12
  112.0 24.0 all-gather.14
  163.8 121.0 all-reduce.4
  287.2 44.5 all-gather.16
  333.4 37.0 all-gather.20
  372.4 31.1 all-gather.18
  419.0 121.0 all-reduce.6
  542.3 34.2 reduce-scatter.13
  700.4 35.1 reduce-scatter.29
  738.2 19.1 reduce-scatter.27
  761.2 44.4 reduce-scatter.25
  808.8 36.7 reduce-scatter.19
  849.0 36.7 reduce-scatter.21
  888.6 35.2 reduce-scatter.15
  927.2 47.0 reduce-scatter.17
  977.5 61.7 reduce-scatter.23
where the time goes:
time: 1060 us; the launch traced here: 1050 us
  waiting for transfers between devices  611 us (58%)
  matrix products  162 us (15%)
  local copies, waits for them, and re-layouts  121 us (11%)
  other arithmetic  75.4 us (7%)
  blocking collectives  51.8 us (5%)
  between operations  16.4 us (2%)
  starting transfers between devices  12.2 us (1%)
    psum x1, waiting for transfers between devices, body(): branch_full = lax.psum(branch_part, 'tp')  116 us
    psum x1, waiting for transfers between devices, body(): d_normed_mid = lax.psum(d_mid_terms, 'tp')  110 us
    reduce_scatter x1, waiting for transfers between devices, body(): lax.psum_scatter(grad_gu.astype(jnp.bfloat16), ('shard', 'ctx'), scatter_...  63 us
    dot_general x24, matrix products, product_t(): lax.dot_general(left, right, (((1,), (1,)), ((), ())), preferred_element_...  58 us
    dot_general x18, matrix products, outer_rows(): lax.dot_general(left, right, (((0,), (0,)), ((), ())), preferred_element_...  52.8 us
    dot_general x18, matrix products, product(): return jnp.dot(left, right, preferred_element_type=jnp.float32)  51.2 us
    reduce_scatter x1, waiting for transfers between devices, body(): lax.psum_scatter(grad_qkv.astype(jnp.bfloat16), ('shard', 'ctx'), scatter...  48.2 us
    all_gather x1, waiting for transfers between devices, body(): lax.all_gather(w_gu, ('shard', 'ctx'), axis=0, tiled=True)  42.5 us
  transfers between devices with their start and end apart: 24, of which 14 were waited for; matrix products, arithmetic and copies ran while one was open for 31% of the time, Pallas kernels for 0%

commit v1 on v0

--- a/solution.py
+++ b/solution.py
@@ -155,7 +155,7 @@
     opener = jax.nn.sigmoid(product(normed, ogate_full))
     gated = (attended_rows * opener).astype(jnp.bfloat16)
     branch_part = product_t(gated, out_full)
-    branch_full = lax.psum(branch_part, "tp")
+    branch_full = lax.all_gather(branch_part, "tp").sum(axis=0)
     middle = residual + branch_full
     middle_share = own_slice(middle)
     normed_mid = norm_rows(middle, gain_mlp).astype(jnp.bfloat16)

time: 1060 us -> 1130 us (1.066)
  waiting for transfers between devices: 611 us -> 672 us
    all_gather x0 -> x1, waiting for transfers between devices: none -> 211 us  [body(): branch_full = lax.all_gather(branch_part, 'tp').sum(axis=0)]
    psum x1 -> x0, waiting for transfers between devices: 116 us -> none  [body(): branch_full = lax.psum(branch_part, 'tp')]
    all_gather x1, waiting for transfers between devices: 42.5 us -> 16.1 us  [body(): lax.all_gather(w_gu, ('shard', 'ctx'), axis=0, tiled=True)]
    unnamed x149 -> x159, local copies, waits for them, and re-layouts: 20.5 us -> 25.2 us
  transfers between devices with their start and end apart: 24 -> 24, of which waited for: 14 -> 14; matrix products, arithmetic and copies ran while one was open for 31% -> 30% of each run, Pallas kernels for 0% -> 0%
where the time goes in v1:
time: 1130 us; the launch traced here: 1120 us
  waiting for transfers between devices  672 us (59%)
  matrix products  158 us (14%)
  local copies, waits for them, and re-layouts  125 us (11%)
  other arithmetic  83.3 us (7%)
  blocking collectives  51.7 us (5%)
  between operations  16.1 us (1%)
  starting transfers between devices  12.2 us (1%)
    all_gather x1, waiting for transfers between devices, body(): branch_full = lax.all_gather(branch_part, 'tp').sum(axis=0)  211 us
    psum x1, waiting for transfers between devices, body(): d_normed_mid = lax.psum(d_mid_terms, 'tp')  110 us
    reduce_scatter x1, waiting for transfers between devices, body(): lax.psum_scatter(grad_gu.astype(jnp.bfloat16), ('shard', 'ctx'), scatter_...  63 us
    dot_general x24, matrix products, product_t(): lax.dot_general(left, right, (((1,), (1,)), ((), ())), preferred_element_...  58 us
    dot_general x18, matrix products, outer_rows(): lax.dot_general(left, right, (((0,), (0,)), ((), ())), preferred_element_...  52.1 us
    reduce_scatter x1, waiting for transfers between devices, body(): lax.psum_scatter(grad_qkv.astype(jnp.bfloat16), ('shard', 'ctx'), scatter...  48.3 us
    dot_general x18, matrix products, product(): return jnp.dot(left, right, preferred_element_type=jnp.float32)  48.2 us
    psum x1, blocking collectives, body(): lax.psum((gain_attn_part, d_gain_mlp_own, jnp.stack([d_query_gain, d_key_...  41.1 us
  transfers between devices with their start and end apart: 24, of which 14 were waited for; matrix products, arithmetic and copies ran while one was open for 30% of the time, Pallas kernels for 0%

profile of v1, /device:TPU:0, one launch (start us, length us, event | category | flops | bytes accessed | tf_op | source)
XLA Modules:
  0.0 1119.1 jit_solution(10644206559586680112)
XLA Ops:
  13.5 10.5 all-gather.1
  26.1 23.3 %all-gather.11.cloned.1.call-done = bf16[1,512,1536]{2,1,0:T(8,128)(2,1)} async-done(((bf16[1,128,1536]{2,1,0:T(8,128)(2,1)}), bf16[1,512,1536]{2,1,0:T(8,128)(2,1)}) %all-gather.11.cloned.1.call-update) | async-done | bytes 1572880 | tf_op jit(solution)/shard_map/all_gather | solution.py:65
  59.5 24.7 %all-gather.13.cloned.1.call-done = bf16[1536,3,384]{2,0,1:T(8,128)(2,1)} async-done(((bf16[192,3,384]{2,0,1:T(8,128)(2,1)}), bf16[1536,3,384]{2,0,1:T(8,128)(2,1)}) %all-gather.13.cloned.1.call-update) | async-done | bytes 3538960 | tf_op jit(solution)/shard_map/all_gather | solution.py:69
  84.2 6.1 copy.92
  90.4 4.1 fusion.41
  96.0 2.9 collective-permute-start
  107.5 3.3 fusion.77
  119.4 37.0 %while.31 = (s32[]{:T(128)}, f32[6,512,64]{1,2,0:T(8,128)}, f32[6,512]{1,0:T(8,128)S(1)}, bf16[6,512,64]{2,1,0:T(8,128)(2,1)}, bf16[6,1024,64]{2,1,0:T(8,128)(2,...) while((s32[]{:T(128)}, f32[6,512,64]{1,2,0:T(8,128)}, ...), condition=%wide.region_8.9_spmd, body=%wide.region_5.8_spmd.sunk | while | flops 139460096 | bytes 7643265 | solution.py:151
  135.5 2.2 fusion.165
  156.9 3.4 fusion.87
  160.4 3.9 fusion.127
  167.3 16.1 %all-gather.19.cloned.1.call-done = bf16[1536,2,1024]{2,0,1:T(8,128)(2,1)} async-done(((bf16[192,2,1024]{2,0,1:T(8,128)(2,1)}), bf16[1536,2,1024]{2,0,1:T(8,128)(2,1)}) %all-gather.19.cloned.1.call-update) | async-done | bytes 6291472 | tf_op jit(solution)/shard_map/all_gather | solution.py:73
  183.4 8.7 copy.104
  192.1 211.0 %all-gather.25.cloned.1.call-done = f32[2048,1536]{1,0:T(8,128)} async-done(((f32[512,1536]{1,0:T(8,128)}), f32[2048,1536]{1,0:T(8,128)}) %all-gather.25.cloned.1.call-update) | async-done | bytes 12582928 | tf_op jit(solution)/shard_map/all_gather | solution.py:158
  403.0 8.0 reduce_sum.192
  411.1 3.0 multiply_reduce_fusion.5
  419.0 5.0 fusion.36
  424.1 15.9 %all-gather.23.cloned.1.call-done = bf16[1,512,1536]{2,1,0:T(8,128)(2,1)} async-done(((bf16[1,128,1536]{2,1,0:T(8,128)(2,1)}), bf16[1,512,1536]{2,1,0:T(8,128)(2,1)}) %all-gather.23.cloned.1.call-update) | async-done | bytes 1572880 | tf_op jit(solution)/shard_map/all_gather | solution.py:66
  439.9 33.1 %all-gather.21.cloned.1.call-done = bf16[1536,1024]{1,0:T(8,128)(2,1)} async-done(((bf16[192,1024]{1,0:T(8,128)(2,1)}), bf16[1536,1024]{1,0:T(8,128)(2,1)}) %all-gather.21.cloned.1.call-update) | async-done | bytes 3145744 | tf_op jit(solution)/shard_map/all_gather | solution.py:74
  473.0 6.0 fusion.55
  480.3 8.0 convolution_bitcast_fusion.2
  493.1 6.6 fusion.50
  500.0 109.6 %all-reduce.4.cloned.1.call-done = f32[512,1536]{1,0:T(8,128)} async-done(((f32[512,1536]{1,0:T(8,128)}), f32[512,1536]{1,0:T(8,128)}) %all-reduce.4.cloned.1.call-update) | async-done | bytes 3145744 | tf_op jit(solution)/shard_map/psum | solution.py:186
  609.6 3.4 multiply_reduce_fusion.1
  613.2 3.0 fusion.43
  621.7 97.3 %while.32 = (s32[]{:T(128)}, f32[6,512,64]{1,2,0:T(8,128)}, f32[6,1024,64]{1,2,0:T(8,128)}, f32[6,1024,64]{1,2,0:T(8,128)}, f32[6,512]{1,0:T(8,128)}, /*index=5*...) while((s32[]{:T(128)}, f32[6,512,64]{1,2,0:T(8,128)}, ...), condition=%wide.region_18.19_spmd, body=%wide.region_14.18_spmd.sunk | while | flops 342981632 | bytes 20376776 | solution.py:216
  736.8 2.3 fusion.83
  742.0 2.7 rev.7
  746.0 4.1 reduce-window.16
  760.8 2.7 rev.8
  765.5 2.6 convolution_convert_fusion.6
  770.3 2.3 multiply_reduce_fusion.6
  777.3 2.3 convolution_bitcast_fusion.3
  781.1 3.6 multiply_reduce_fusion.2
  785.5 6.3 convolution_convert_fusion.2
  791.9 3.6 convolution_convert_fusion.5
  798.6 5.8 convolution_convert_fusion.1
  804.5 3.1 maximum_convert_fusion
  807.6 3.9 copy.114
  811.6 8.2 convolution_convert_fusion
  824.5 41.1 %all-reduce.1 = (f32[24]{0:T(128)}, f32[1536]{0:T(1024)}, f32[1536]{0:T(1024)}, f32[2,64]{1,0:T(2,128)}) all-reduce(f32[24]{0:T(128)S(1)} %dynamic_update_slice.28, f32[1536]{0:T(1024)S(1)} %get-tuple-element.207, f32[1536]{0:T(1024)S(1)} %fusion.109, ...), channel_id=1, replica_groups=mesh['shard'=4,'ctx'=2,'tp'=4] {'shard','ctx','tp'}, use_global_device_ids=true, to_apply=%region_30.31 | all-reduce | flops 3224 | bytes 25792 | tf_op jit(solution)/shard_map/psum | solution.py:308
  866.5 8.9 reduce-scatter.26.cloned.1.call-done
  877.4 37.9 %reduce-scatter.20.cloned.1.call-done = bf16[192,384]{1,0:T(8,128)(2,1)} async-done(((bf16[1536,384]{1,0:T(8,128)(2,1)}), bf16[192,384]{1,0:T(8,128)(2,1)}) %reduce-scatter.20.cloned.1.call-update) | async-done | bytes 147472 | tf_op jit(solution)/shard_map/reduce_scatter | solution.py:291
  917.0 38.6 %reduce-scatter.22.cloned.1.call-done = bf16[192,384]{1,0:T(8,128)(2,1)} async-done(((bf16[1536,384]{1,0:T(8,128)(2,1)}), bf16[192,384]{1,0:T(8,128)(2,1)}) %reduce-scatter.22.cloned.1.call-update) | async-done | bytes 147472 | tf_op jit(solution)/shard_map/reduce_scatter | solution.py:294
  957.2 36.4 %reduce-scatter.16.cloned.1.call-done = bf16[1,128,1536]{2,1,0:T(8,128)(2,1)} async-done(((bf16[1,512,1536]{2,1,0:T(8,128)(2,1)}), bf16[1,128,1536]{2,1,0:T(8,128)(2,1)}) %reduce-scatter.16.cloned.1.call-update) | async-done | bytes 393232 | tf_op jit(solution)/shard_map/reduce_scatter | solution.py:269
  995.8 48.3 %reduce-scatter.18.cloned.1.call-done = bf16[192,3,384]{2,0,1:T(8,128)(2,1)} async-done(((bf16[1536,3,384]{2,0,1:T(8,128)(2,1)}), bf16[192,3,384]{2,0,1:T(8,128)(2,1)}) %reduce-scatter.18.cloned.1.call-update) | async-done | bytes 442384 | tf_op jit(solution)/shard_map/reduce_scatter | solution.py:285
  1046.0 63.0 %reduce-scatter.24.cloned.1.call-done = bf16[192,2,1024]{2,0,1:T(8,128)(2,1)} async-done(((bf16[1536,2,1024]{2,0,1:T(8,128)(2,1)}), bf16[192,2,1024]{2,0,1:T(8,128)(2,1)}) %reduce-scatter.24.cloned.1.call-update) | async-done | bytes 786448 | tf_op jit(solution)/shard_map/reduce_scatter | solution.py:297
  1109.0 3.1 copy.116
  (431 shorter events, 250.0 us)
Async XLA Ops:
  7.2 5.3 copy-start.72
  7.2 6.3 copy-start.70
  7.2 42.2 %all-gather.11.cloned.1.call-start = ((), (), s32[]{:S(2)}) async-start(), calls=%async_computation.9 | async-start | bytes 1966080 | tf_op jit(solution)/shard_map/all_gather | solution.py:65
  7.9 76.3 %all-gather.13.cloned.1.call-start = ((), (), s32[]{:S(2)}) async-start(), calls=%async_computation.10 | async-start | bytes 3981312 | tf_op jit(solution)/shard_map/all_gather | solution.py:69
  8.7 147.7 %all-gather.15.cloned.1.call-start = ((), (), s32[]{:S(2)}) async-start(), calls=%async_computation.11 | async-start | bytes 1327104 | tf_op jit(solution)/shard_map/all_gather | solution.py:71
  9.4 151.0 %all-gather.17.cloned.1.call-start = ((), (), s32[]{:S(2)}) async-start(), calls=%async_computation.12 | async-start | bytes 1327104 | tf_op jit(solution)/shard_map/all_gather | solution.py:72
  10.0 16.0 %copy-start.74 = (f32[24]{0:T(128)S(1)}, f32[24]{0:T(128)}, u32[]{:S(2)}) copy-start(f32[24]{0:T(128)} %param.24) | copy-start | bytes 292
  10.0 173.4 %all-gather.19.cloned.1.call-start = ((), (), s32[]{:S(2)}) async-start(), calls=%async_computation.13 | async-start | bytes 7077888 | tf_op jit(solution)/shard_map/all_gather | solution.py:73
  12.3 38.9 %copy-start.62 = (f32[1536]{0:T(1024)S(1)}, f32[1536]{0:T(1024)}, u32[]{:S(2)}) copy-start(f32[1536]{0:T(1024)} %param.29) | copy-start | bytes 18436
  12.3 390.7 %all-gather.25.cloned.1.call-start = ((), (), s32[]{:S(2)}) async-start(), calls=%async_computation.24 | async-start | bytes 15728640 | tf_op jit(solution)/shard_map/all_gather | solution.py:158
  13.1 81.7 %copy-start.54 = (f32[384]{0:T(512)}, f32[384]{0:T(512)S(1)}, u32[]{:S(2)}) copy-start(f32[384]{0:T(512)S(1)} %mul.523) | copy-start | bytes 4612
  24.1 29.1 %copy-start.42 = (bf16[1536,6]{0,1:T(8,128)(2,1)}, bf16[1536,6]{0,1:T(8,128)(2,1)S(1)}, u32[]{:S(2)}) copy-start(bf16[1536,6]{0,1:T(8,128)(2,1)S(1)} %reshape.801) | copy-start | bytes 55300
  51.2 39.1 %copy-start.60 = (f32[512]{0:T(512)}, f32[512]{0:T(512)S(1)}, u32[]{:S(2)}) copy-start(f32[512]{0:T(512)S(1)} %add_rsqrt_fusion) | copy-start | bytes 6148
  53.3 5.0 copy-start.47
  55.6 2.4 collective-permute-start.1
  59.5 30.9 %copy-start.2 = (bf16[1,512,1536]{2,1,0:T(8,128)(2,1)S(1)}, bf16[1,512,1536]{2,1,0:T(8,128)(2,1)}, u32[]{:S(2)}) copy-start(bf16[1,512,1536]{2,1,0:T(8,128)(2,1)} %all-gather.11.cloned.1.call-done) | copy-start | bytes 4718596
  94.5 8.5 copy-start.6
  94.6 8.4 copy-start.11
  94.6 10.1 copy-start.8
  94.8 7.0 copy-start.38
  96.0 14.8 %collective-permute-start = (bf16[1,512,384]{1,2,0:T(8,128)(2,1)}, bf16[1,512,384]{1,2,0:T(8,128)(2,1)}, u32[]{:S(2)}, u32[]{:S(2)}) collective-permute-start(bf16[1,512,384]{1,2,0:T(8,128)(2,1)} %multiply_convert_fusion.8), channel_id=1, source_target_pairs={{0,4},{1,5},{2,6},{3,7},{8,12},{9,13},{10,14},{11,15},{16,20},{17,... | collective-permute-start | bytes 1179656 | tf_op jit(solution)/shard_map/ppermute | solution.py:13
  99.7 13.3 %collective-permute-start.2 = (bf16[1,512,384]{1,2,0:T(8,128)(2,1)}, bf16[1,512,384]{1,2,0:T(8,128)(2,1)}, u32[]{:S(2)}, u32[]{:S(2)}) collective-permute-start(bf16[1,512,384]{1,2,0:T(8,128)(2,1)} %slice_bitcast_fusion.5), channel_id=1, source_target_pairs={{0,4},{1,5},{2,6},{3,7},{8,12},{9,13},{10,14},{11,15},{16,20},{17,... | collective-permute-start | bytes 1179656 | tf_op jit(solution)/shard_map/ppermute | solution.py:13
  164.4 275.6 %all-gather.23.cloned.1.call-start = ((), (), s32[]{:S(2)}) async-start(), calls=%async_computation.16 | async-start | bytes 1966080 | tf_op jit(solution)/shard_map/all_gather | solution.py:66
  165.1 307.9 %all-gather.21.cloned.1.call-start = ((), (), s32[]{:S(2)}) async-start(), calls=%async_computation.14 | async-start | bytes 3538944 | tf_op jit(solution)/shard_map/all_gather | solution.py:74
  165.9 443.7 %all-reduce.4.cloned.1.call-start = ((), (), s32[]{:S(2)}) async-start(), calls=%async_computation.17 | async-start | bytes 6291456 | tf_op jit(solution)/shard_map/psum | solution.py:186
  411.1 4.5 copy-start.1
  411.1 4.5 copy-start.3
  411.1 4.5 copy-start.44
  414.1 195.5 %copy-start = (f32[512,1536]{1,0:T(8,128)}, f32[512,1536]{1,0:T(8,128)S(1)}, u32[]{:S(2)}) copy-start(f32[512,1536]{1,0:T(8,128)S(1)} %get-tuple-element.267) | copy-start | bytes 9437188
  488.4 332.2 %reduce-scatter.14.cloned.1.call-start = ((), (), s32[]{:S(2)}) async-start(), calls=%async_computation.15 | async-start | bytes 1966080 | tf_op jit(solution)/shard_map/reduce_scatter | solution.py:167
  499.7 323.2 %reduce-scatter.30.cloned.1.call-start = ((), (), s32[]{:S(2)}) async-start(), calls=%async_computation.26 | async-start | bytes 442368
  723.0 51.9 %collective-permute-start.4 = (bf16[1,512,384]{1,2,0:T(8,128)(2,1)}, bf16[1,512,384]{1,2,0:T(8,128)(2,1)}, u32[]{:S(2)}, u32[]{:S(2)}) collective-permute-start(bf16[1,512,384]{1,2,0:T(8,128)(2,1)} %bitcast.103), channel_id=1, source_target_pairs={{4,0},{5,1},{6,2},{7,3},{12,8},{13,9},{14,10},{15,11},{20,16},{21,... | collective-permute-start | bytes 1179656 | tf_op jit(solution)/shard_map/ppermute | solution.py:13
  726.2 44.0 %collective-permute-start.3 = (bf16[1,512,384]{1,2,0:T(8,128)(2,1)}, bf16[1,512,384]{1,2,0:T(8,128)(2,1)}, u32[]{:S(2)}, u32[]{:S(2)}) collective-permute-start(bf16[1,512,384]{1,2,0:T(8,128)(2,1)} %bitcast.93), channel_id=1, source_target_pairs={{4,0},{5,1},{6,2},{7,3},{12,8},{13,9},{14,10},{15,11},{20,16},{21,... | collective-permute-start | bytes 1179656 | tf_op jit(solution)/shard_map/ppermute | solution.py:13
  735.4 5.1 copy-start.28
  735.4 6.0 copy-start.37
  735.4 6.0 copy-start.41
  735.4 6.0 collective-permute-start.5
  769.8 95.9 %reduce-scatter.28.cloned.1.call-start = ((), (), s32[]{:S(2)}) async-start(), calls=%async_computation.25 | async-start | bytes 163840
  774.8 4.7 copy-start.30
  774.9 4.7 copy-start.32
  785.4 90.0 %reduce-scatter.26.cloned.1.call-start = ((), (), s32[]{:S(2)}) async-start(), calls=%async_computation.23 | async-start | bytes 3538944 | tf_op jit(solution)/shard_map/reduce_scatter | solution.py:300
  791.8 123.5 %reduce-scatter.20.cloned.1.call-start = ((), (), s32[]{:S(2)}) async-start(), calls=%async_computation.20 | async-start | bytes 1327104 | tf_op jit(solution)/shard_map/reduce_scatter | solution.py:291
  795.5 160.0 %reduce-scatter.22.cloned.1.call-start = ((), (), s32[]{:S(2)}) async-start(), calls=%async_computation.21 | async-start | bytes 1327104 | tf_op jit(solution)/shard_map/reduce_scatter | solution.py:294
  797.7 195.9 %reduce-scatter.16.cloned.1.call-start = ((), (), s32[]{:S(2)}) async-start(), calls=%async_computation.18 | async-start | bytes 1966080 | tf_op jit(solution)/shard_map/reduce_scatter | solution.py:269
  798.3 245.8 %reduce-scatter.18.cloned.1.call-start = ((), (), s32[]{:S(2)}) async-start(), calls=%async_computation.19 | async-start | bytes 3981312 | tf_op jit(solution)/shard_map/reduce_scatter | solution.py:285
  804.5 304.5 %reduce-scatter.24.cloned.1.call-start = ((), (), s32[]{:S(2)}) async-start(), calls=%async_computation.22 | async-start | bytes 7077888 | tf_op jit(solution)/shard_map/reduce_scatter | solution.py:297
  819.8 4.6 copy-start.59
  819.8 4.7 copy-start.71
  (56 other events, 123.4 us)
Sparse Core Ops, SparseCore 0:
  9.6 39.7 all-gather.10
  51.3 32.8 all-gather.12
  86.1 24.0 all-gather.14
  112.0 24.0 all-gather.16
  137.8 45.5 all-gather.18
  184.8 218.1 all-gather.24
  404.6 35.2 all-gather.22
  441.8 31.1 all-gather.20
  488.5 121.0 all-reduce.3
  611.7 34.2 reduce-scatter.13
  769.9 35.1 reduce-scatter.29
  807.8 19.1 reduce-scatter.27
  830.7 44.6 reduce-scatter.25
  878.5 36.7 reduce-scatter.19
  918.7 36.7 reduce-scatter.21
  958.3 35.2 reduce-scatter.15
  996.9 47.0 reduce-scatter.17
  1047.2 61.6 reduce-scatter.23
